TPU v7x, 32 devices: a whole 2x2x4 slice. The times are simulated.
32 devices in a mesh: seg: 4 (over y, core), sec: 8 (over z, x).
Axes of the slice: x: 2, y: 2, z: 4, core: 2. Of those that a mesh axis runs over, the one named last changes fastest.
Arguments:
- wavefunction: bfloat16 [4, 8, 256, 256], P('seg'), may hold values from -6 to 6
- left_env: bfloat16 [4, 32, 8, 256, 256], P('seg', 'sec'), may hold values from -0.375 to 0.375
- right_env: bfloat16 [4, 32, 8, 256, 256], P('seg', 'sec'), may hold values from -0.375 to 0.375
- block_sizes: int32 [4, 8], P('seg'), may hold values from 64 to 256, as said below
Outputs:
- new_wavefunction: bfloat16 [4, 8, 256, 256], P('seg')
- incoming_left_env: bfloat16 [4, 32, 8, 256, 256], P('seg', 'sec')
- incoming_right_env: bfloat16 [4, 32, 8, 256, 256], P('seg', 'sec')
Inputs may be any that keep to these rules, and one draw needn't show every extreme that they name: `block_sizes`: every block size is a multiple of 64; some block has size 256.
All inputs are finite; a program needn't handle non-finite values.
Results may differ from a plain program's by a relative error of at most 0.035.
Values may be sent and summed in bfloat16 or wider, within the bound.
No kernel may reach another device: no remote copies, remote signals or barrier semaphores. Data moves between devices by JAX's collectives and lax.ppermute only.
A program may use at most 64 MiB of HBM per device.

v0:
```python
import jax
import jax.numpy as jnp
from jax import lax
from jax.sharding import PartitionSpec as P

ITERS = 4
epsilon = 1e-06


def passed_along(block, axis, distance):
    devices = range(lax.axis_size(axis))
    route = [(i - distance, i) for i in devices if i - distance in devices]
    return lax.ppermute(block, axis, route)


def body(wavefunction, left_env, right_env, block_sizes):
    left_local = left_env[0]
    right_local = right_env[0]
    blocks = left_local.shape[3]
    groups = lax.axis_size("sec")
    channels = left_local.shape[0] * groups
    sizes = block_sizes[0]
    index = jnp.arange(blocks)
    live = (index[:, None] < sizes[None, :]).astype(jnp.float32)
    mask = live[:, :, None] * jnp.transpose(live)[None, :, :]
    start = jnp.transpose(wavefunction[0], (1, 0, 2)).astype(jnp.float32) * mask
    state_tensor = (start / jnp.sqrt(jnp.mean(start * start) + epsilon)).astype(jnp.bfloat16)
    root_channels = jnp.sqrt(jnp.float32(channels))
    for iteration in range(ITERS):
        state_f = state_tensor.astype(jnp.float32)
        product = jnp.einsum(
            "wkab,bkc->wkac", left_local, state_tensor, preferred_element_type=jnp.float32
        ).astype(jnp.bfloat16)
        applied = (
            lax.psum(
                jnp.einsum(
                    "wkac,wkcd->akd", product, right_local, preferred_element_type=jnp.float32
                ).astype(jnp.bfloat16),
                "sec",
            ).astype(jnp.float32)
            / root_channels
        )
        theta = jnp.sum(state_f * applied) / jnp.sum(state_f * state_f)
        update = mask * (state_f - (applied - theta * state_f))
        state_tensor = (update / jnp.sqrt(jnp.mean(update * update) + epsilon)).astype(jnp.bfloat16)
    scale_factor = jnp.sqrt(jnp.float32(blocks))
    left_portion = jnp.einsum(
        "akc,wkab->wkcb", state_tensor, left_local, preferred_element_type=jnp.float32
    ).astype(jnp.bfloat16)
    built_left = (
        jnp.einsum("gxah,hxe->gxae", left_portion, state_tensor, preferred_element_type=jnp.float32)
        / scale_factor
    ).astype(jnp.bfloat16)
    incoming_left_env = passed_along(built_left[None], "seg", 1)
    right_portion = jnp.einsum(
        "akc,wkcd->wkad", state_tensor, right_local, preferred_element_type=jnp.float32
    ).astype(jnp.bfloat16)
    built_right = (
        jnp.einsum(
            "njpq,tjq->njpt", right_portion, state_tensor, preferred_element_type=jnp.float32
        )
        / scale_factor
    ).astype(jnp.bfloat16)
    incoming_right_env = passed_along(built_right[None], "seg", -1)
    new_wave = jnp.transpose(state_tensor, (1, 0, 2))[None]
    return (new_wave, incoming_left_env, incoming_right_env)


def solution(mesh):
    placed = (
        P("seg", None, None, None),
        P("seg", "sec", None, None, None),
        P("seg", "sec", None, None, None),
        P("seg", None),
    )
    return jax.shard_map(
        body,
        mesh=mesh,
        in_specs=placed,
        out_specs=(
            P("seg", None, None, None),
            P("seg", "sec", None, None, None),
            P("seg", "sec", None, None, None),
        ),
        check_vma=False,
    )
```

profile of v0, /device:TPU:1, one launch (start us, length us, event | category | flops | bytes accessed | tf_op | source)
XLA Modules:
  0.0 461.6 jit_solution(12130565121797320660)
XLA Ops:
  7.2 0.0 all-reduce.5.cloned.1.call-start
  7.2 0.7 fusion.133
  7.9 0.7 fusion.132
  8.7 2.5 fusion.66
  11.8 0.0 copy-start
  11.8 7.3 %fusion.92 = bf16[256,8,256]{2,0,1:T(8,128)(2,1)} fusion(bf16[1,4,8,256,256]{4,3,2,1,0:T(8,128)(2,1)} %param.6, bf16[1,4,8,256,256]{4,3,2,1,0:T(8,128)(2,1)} %param.5, bf16[1,8,256,256]{3,2,1,0:T(8,128)(2,1)} %param.4, f32[]{:T(128)S(6)} %sqrt.15, f32[8,256]{1,0:T(8,128)S(1)} %fusion.133, f32[256,8]{0,1:T(8,128)S(1)} %fusion.132), kind=kOutput, calls=%fused_computation.92 | convolution fusion | flops 2152726528 | bytes 10502148 | tf_op jit(solution)/shard_map/wkac,wkcd->akd/dot_general | solution.py:36
  19.1 0.0 all-reduce.5.cloned.1.call-update
  19.1 0.0 all-reduce.7.cloned.1.call-start
  19.2 80.3 %all-reduce.5.cloned.1.call-done = bf16[256,8,256]{2,0,1:T(8,128)(2,1)} async-done(((bf16[256,8,256]{2,0,1:T(8,128)(2,1)}), bf16[256,8,256]{2,0,1:T(8,128)(2,1)}) %all-reduce.5.cloned.1.call-update) | async-done | bytes 1048592 | tf_op jit(solution)/shard_map/psum | solution.py:35
  99.5 0.0 copy-done
  99.5 0.0 copy-start.1
  99.5 2.9 fusion.53
  103.7 0.0 copy-done.1
  103.7 1.7 multiply_reduce_fusion.3
  106.1 0.8 divide_convert_fusion.3
  106.9 6.8 %fusion.99 = bf16[256,8,256]{2,0,1:T(8,128)(2,1)} fusion(bf16[256,8,256]{2,0,1:T(8,128)(2,1)S(1)} %divide_convert_fusion.3, bf16[1,4,8,256,256]{4,3,2,1,0:T(8,128)(2,1)} %param.6, bf16[1,4,8,256,256]{4,3,2,1,0:T(8,128)(2,1)} %param.5), kind=kOutput, calls=%fused_computation.93 | convolution fusion | flops 2150105088 | bytes 10485760 | tf_op jit(solution)/shard_map/wkac,wkcd->akd/dot_general | solution.py:36
  113.7 0.0 all-reduce.7.cloned.1.call-update
  113.8 0.2 all-reduce.9.cloned.1.call-start
  114.0 77.8 %all-reduce.7.cloned.1.call-done = bf16[256,8,256]{2,0,1:T(8,128)(2,1)} async-done(((bf16[256,8,256]{2,0,1:T(8,128)(2,1)}), bf16[256,8,256]{2,0,1:T(8,128)(2,1)}) %all-reduce.7.cloned.1.call-update) | async-done | bytes 1048592 | tf_op jit(solution)/shard_map/psum | solution.py:35
  191.8 0.0 copy-start.3
  191.8 2.5 fusion.56
  195.6 0.0 copy-done.3
  195.6 1.5 multiply_reduce_fusion.2
  197.8 0.7 divide_convert_fusion.2
  198.5 6.8 %fusion.106 = bf16[256,8,256]{2,0,1:T(8,128)(2,1)} fusion(bf16[256,8,256]{2,0,1:T(8,128)(2,1)S(1)} %divide_convert_fusion.2, bf16[1,4,8,256,256]{4,3,2,1,0:T(8,128)(2,1)} %param.6, bf16[1,4,8,256,256]{4,3,2,1,0:T(8,128)(2,1)} %param.5), kind=kOutput, calls=%fused_computation.94 | convolution fusion | flops 2150105088 | bytes 10485760 | tf_op jit(solution)/shard_map/wkac,wkcd->akd/dot_general | solution.py:36
  205.3 0.0 all-reduce.9.cloned.1.call-update
  205.3 0.0 all-reduce.11.cloned.1.call-start
  205.3 77.8 %all-reduce.9.cloned.1.call-done = bf16[256,8,256]{2,0,1:T(8,128)(2,1)} async-done(((bf16[256,8,256]{2,0,1:T(8,128)(2,1)}), bf16[256,8,256]{2,0,1:T(8,128)(2,1)}) %all-reduce.9.cloned.1.call-update) | async-done | bytes 1048592 | tf_op jit(solution)/shard_map/psum | solution.py:35
  283.2 0.0 copy-start.4
  283.2 2.5 fusion.59
  287.0 0.0 copy-done.4
  287.0 1.5 multiply_reduce_fusion.1
  289.2 0.7 divide_convert_fusion.1
  289.9 6.8 %fusion.113 = bf16[256,8,256]{2,0,1:T(8,128)(2,1)} fusion(bf16[256,8,256]{2,0,1:T(8,128)(2,1)S(1)} %divide_convert_fusion.1, bf16[1,4,8,256,256]{4,3,2,1,0:T(8,128)(2,1)} %param.6, bf16[1,4,8,256,256]{4,3,2,1,0:T(8,128)(2,1)} %param.5), kind=kOutput, calls=%fused_computation.95 | convolution fusion | flops 2150105088 | bytes 10485760 | tf_op jit(solution)/shard_map/wkac,wkcd->akd/dot_general | solution.py:36
  296.6 0.0 all-reduce.11.cloned.1.call-update
  296.7 78.0 %all-reduce.11.cloned.1.call-done = bf16[256,8,256]{2,0,1:T(8,128)(2,1)} async-done(((bf16[256,8,256]{2,0,1:T(8,128)(2,1)}), bf16[256,8,256]{2,0,1:T(8,128)(2,1)}) %all-reduce.11.cloned.1.call-update) | async-done | bytes 1048592 | tf_op jit(solution)/shard_map/psum | solution.py:35
  374.7 0.0 copy-start.2
  374.7 2.5 fusion.62
  378.5 0.0 copy-done.2
  378.5 1.5 multiply_reduce_fusion
  380.7 0.7 divide_convert_fusion
  381.4 0.0 copy-start.5
  381.4 7.1 %fusion = bf16[1,4,8,256,256]{3,4,1,2,0:T(8,128)(2,1)} fusion(bf16[256,8,256]{2,0,1:T(8,128)(2,1)S(1)} %divide_convert_fusion, bf16[1,4,8,256,256]{4,3,2,1,0:T(8,128)(2,1)} %param.5), kind=kOutput, calls=%fused_computation.7 | convolution fusion | flops 2153775104 | bytes 9437184 | tf_op jit(solution)/shard_map/gxah,hxe->gxae/dot_general | solution.py:51
  388.5 3.7 collective-permute-start
  392.2 0.0 copy-done.5
  392.2 6.5 %fusion.1 = bf16[1,4,8,256,256]{3,4,1,2,0:T(8,128)(2,1)} fusion(bf16[256,8,256]{2,0,1:T(8,128)(2,1)S(1)} %divide_convert_fusion, bf16[1,4,8,256,256]{4,3,2,1,0:T(8,128)(2,1)} %param.6), kind=kOutput, calls=%fused_computation.8 | convolution fusion | flops 2153775104 | bytes 9437184 | tf_op jit(solution)/shard_map/njpq,tjq->njpt/dot_general | solution.py:59
  398.7 2.5 collective-permute-start.1
  401.3 36.7 %collective-permute-done = bf16[1,4,8,256,256]{3,4,1,2,0:T(8,128)(2,1)} collective-permute-done((bf16[1,4,8,256,256]{3,4,1,2,0:T(8,128)(2,1)}, bf16[1,4,8,256,256]{3,4,1,2,0:T(8,128)(2,1)}, u32[]{:S(2)}, u32[]{:S(2)}) %collective-permute-start) | collective-permute-done | bytes 4194336 | tf_op jit(solution)/shard_map/ppermute | solution.py:13
  438.0 6.2 %copy.12 = bf16[1,4,8,256,256]{4,3,2,1,0:T(8,128)(2,1)} copy(bf16[1,4,8,256,256]{3,4,1,2,0:T(8,128)(2,1)} %collective-permute-done) | data formatting | bytes 8388608
  444.1 4.7 %collective-permute-done.1 = bf16[1,4,8,256,256]{3,4,1,2,0:T(8,128)(2,1)} collective-permute-done((bf16[1,4,8,256,256]{3,4,1,2,0:T(8,128)(2,1)}, bf16[1,4,8,256,256]{3,4,1,2,0:T(8,128)(2,1)}, u32[]{:S(2)}, u32[]{:S(2)}) %collective-permute-start.1) | collective-permute-done | bytes 4194336 | tf_op jit(solution)/shard_map/ppermute | solution.py:13
  448.9 6.2 %copy.13 = bf16[1,4,8,256,256]{4,3,2,1,0:T(8,128)(2,1)} copy(bf16[1,4,8,256,256]{3,4,1,2,0:T(8,128)(2,1)} %collective-permute-done.1) | data formatting | bytes 8388608
Async XLA Ops:
  7.2 92.3 %all-reduce.5.cloned.1.call-start = ((), (), s32[]{:S(2)}) async-start(), calls=%async_computation | async-start | bytes 2097152 | tf_op jit(solution)/shard_map/psum | solution.py:35
  11.8 87.6 %copy-start = (bf16[1,8,256,256]{3,2,1,0:T(8,128)(2,1)S(1)}, bf16[1,8,256,256]{3,2,1,0:T(8,128)(2,1)}, u32[]{:S(2)}) copy-start(bf16[1,8,256,256]{3,2,1,0:T(8,128)(2,1)} %param.4) | copy-start | bytes 3145732
  19.1 172.6 %all-reduce.7.cloned.1.call-start = ((), (), s32[]{:S(2)}) async-start(), calls=%async_computation.1 | async-start | bytes 2097152 | tf_op jit(solution)/shard_map/psum | solution.py:35
  99.5 4.2 copy-start.1
  113.8 169.4 %all-reduce.9.cloned.1.call-start = ((), (), s32[]{:S(2)}) async-start(), calls=%async_computation.2 | async-start | bytes 2097152 | tf_op jit(solution)/shard_map/psum | solution.py:35
  191.8 3.8 copy-start.3
  205.3 169.4 %all-reduce.11.cloned.1.call-start = ((), (), s32[]{:S(2)}) async-start(), calls=%async_computation.3 | async-start | bytes 2097152 | tf_op jit(solution)/shard_map/psum | solution.py:35
  283.2 3.8 copy-start.4
  374.7 3.8 copy-start.2
  381.4 10.8 %copy-start.5 = (bf16[256,8,256]{2,0,1:T(8,128)(2,1)}, bf16[256,8,256]{2,0,1:T(8,128)(2,1)S(1)}, u32[]{:S(2)}) copy-start(bf16[256,8,256]{2,0,1:T(8,128)(2,1)S(1)} %divide_convert_fusion) | copy-start | bytes 3145732
  388.5 49.5 %collective-permute-start = (bf16[1,4,8,256,256]{3,4,1,2,0:T(8,128)(2,1)}, bf16[1,4,8,256,256]{3,4,1,2,0:T(8,128)(2,1)}, u32[]{:S(2)}, u32[]{:S(2)}) collective-permute-start(bf16[1,4,8,256,256]{3,4,1,2,0:T(8,128)(2,1)} %fusion), channel_id=1, source_target_pairs={{0,8},{8,16},{16,24},{1,9},{9,17},{17,25},{2,10},{10,18},{18,26},{... | collective-permute-start | bytes 12582920 | tf_op jit(solution)/shard_map/ppermute | solution.py:13
  398.7 50.1 %collective-permute-start.1 = (bf16[1,4,8,256,256]{3,4,1,2,0:T(8,128)(2,1)}, bf16[1,4,8,256,256]{3,4,1,2,0:T(8,128)(2,1)}, u32[]{:S(2)}, u32[]{:S(2)}) collective-permute-start(bf16[1,4,8,256,256]{3,4,1,2,0:T(8,128)(2,1)} %fusion.1), channel_id=1, source_target_pairs={{8,0},{16,8},{24,16},{9,1},{17,9},{25,17},{10,2},{18,10},{26,18},{... | collective-permute-start | bytes 12582920 | tf_op jit(solution)/shard_map/ppermute | solution.py:13
Sparse Core Ops, SparseCore 0:
  19.3 80.1 all-reduce.4
  113.9 77.8 all-reduce.6
  205.4 77.7 all-reduce.8
  296.8 77.8 all-reduce.10
where the time goes:
time: 462 us
  waiting for transfers between devices  355 us (77%)
  matrix products  41.2 us (9%)
  other arithmetic  23.3 us (5%)
  between operations  22.7 us (5%)
  local copies, waits for them, and re-layouts  12.4 us (3%)
  starting transfers between devices  6.56 us (1%)
    psum x4, waiting for transfers between devices, body(): lax.psum(jnp.einsum('wkac,wkcd->akd', product, right_local, preferred_ele...  314 us
    ppermute x2, waiting for transfers between devices, passed_along(): return lax.ppermute(block, axis, route)  41.4 us
    dot_general x4, matrix products, body(): jnp.einsum('wkac,wkcd->akd', product, right_local, preferred_element_type...  27.6 us
    unnamed x14, local copies, waits for them, and re-layouts  12.4 us
    reduce_sum x4, other arithmetic, body(): theta = jnp.sum(state_f * applied) / jnp.sum(state_f * state_f)  10.3 us
  transfers between devices with their start and end apart: 6, of which 6 were waited for; matrix products, arithmetic and copies ran while one was open for 3% of the time, Pallas kernels for 0%

commit v1 on v0

--- a/solution.py
+++ b/solution.py
@@ -5,6 +5,11 @@
 
 ITERS = 4
 epsilon = 1e-06
+
+
+def summed_here(x, axis):
+    parts = lax.all_gather(x, axis)
+    return jnp.sum(parts, axis=0)
 
 
 def passed_along(block, axis, distance):
@@ -32,7 +37,7 @@
             "wkab,bkc->wkac", left_local, state_tensor, preferred_element_type=jnp.float32
         ).astype(jnp.bfloat16)
         applied = (
-            lax.psum(
+            summed_here(
                 jnp.einsum(
                     "wkac,wkcd->akd", product, right_local, preferred_element_type=jnp.float32
                 ).astype(jnp.bfloat16),

time: 462 us -> 677 us (1.47)
  waiting for transfers between devices: 355 us -> 532 us
  other arithmetic: 23.3 us -> 57.3 us
    all_gather x0 -> x4, waiting for transfers between devices: none -> 494 us  [summed_here(): parts = lax.all_gather(x, axis)]
    psum x4 -> x0, waiting for transfers between devices: 314 us -> none  [body(): lax.psum(jnp.einsum('wkac,wkcd->akd', product, right_local, preferred_ele...]
    reduce_sum x0 -> x4, other arithmetic: none -> 22.1 us  [summed_here(): return jnp.sum(parts, axis=0)]
where the time goes in v1:
time: 677 us; the launch traced here: 676 us
  waiting for transfers between devices  532 us (79%)
  other arithmetic  57.3 us (8%)
  matrix products  45.6 us (7%)
  between operations  22.7 us (3%)
  local copies, waits for them, and re-layouts  12.4 us (2%)
  starting transfers between devices  6.84 us (1%)
    all_gather x4, waiting for transfers between devices, summed_here(): parts = lax.all_gather(x, axis)  494 us
    ppermute x2, waiting for transfers between devices, passed_along(): return lax.ppermute(block, axis, route)  37.5 us
    dot_general x4, matrix products, body(): jnp.einsum('wkac,wkcd->akd', product, right_local, preferred_element_type...  28.5 us
    reduce_sum x4, other arithmetic, summed_here(): return jnp.sum(parts, axis=0)  22.1 us
  transfers between devices with their start and end apart: 6, of which 6 were waited for; matrix products, arithmetic and copies ran while one was open for 3% of the time, Pallas kernels for 0%

profile of v1, /device:TPU:1, one launch (start us, length us, event | category | flops | bytes accessed | tf_op | source)
XLA Modules:
  0.0 676.5 jit_solution(15733584605304724718)
XLA Ops:
  7.2 0.0 all-gather.9.cloned.1.call-start
  7.2 0.7 fusion.147
  7.9 0.7 fusion.148
  8.7 2.5 fusion.58
  11.8 7.2 %fusion.106 = bf16[256,8,256]{2,0,1:T(8,128)(2,1)} fusion(bf16[1,4,8,256,256]{4,3,2,1,0:T(8,128)(2,1)} %param.6, bf16[1,4,8,256,256]{4,3,2,1,0:T(8,128)(2,1)} %param.5, bf16[1,8,256,256]{3,2,1,0:T(8,128)(2,1)} %param.4, f32[]{:T(128)S(6)} %sqrt.15, f32[8,256]{1,0:T(8,128)S(1)} %fusion.147, f32[256,8]{0,1:T(8,128)S(1)} %fusion.148), kind=kOutput, calls=%fused_computation.119 | convolution fusion | flops 2152726528 | bytes 10502148 | tf_op jit(solution)/shard_map/wkac,wkcd->akd/dot_general | solution.py:41
  19.0 0.0 all-gather.9.cloned.1.call-update
  19.1 0.0 all-gather.11.cloned.1.call-start
  19.1 125.9 %all-gather.9.cloned.1.call-done = bf16[2048,8,256]{2,0,1:T(8,128)(2,1)} async-done(((bf16[256,8,256]{2,0,1:T(8,128)(2,1)}), bf16[2048,8,256]{2,0,1:T(8,128)(2,1)}) %all-gather.9.cloned.1.call-update) | async-done | bytes 8388624 | tf_op jit(solution)/shard_map/all_gather | solution.py:11
  145.0 0.0 copy-start
  145.0 5.0 reduce_sum.166
  150.0 0.0 copy-done
  150.0 1.5 fusion.61
  152.9 1.7 multiply_reduce_fusion.3
  155.3 0.8 divide_convert_fusion.3
  156.2 0.0 copy-start.1
  156.2 7.1 %fusion.113 = bf16[256,8,256]{2,0,1:T(8,128)(2,1)} fusion(bf16[256,8,256]{2,0,1:T(8,128)(2,1)S(1)} %divide_convert_fusion.3, bf16[1,4,8,256,256]{4,3,2,1,0:T(8,128)(2,1)} %param.6, bf16[1,4,8,256,256]{4,3,2,1,0:T(8,128)(2,1)} %param.5), kind=kOutput, calls=%fused_computation.120 | convolution fusion | flops 2150105088 | bytes 10485760 | tf_op jit(solution)/shard_map/wkac,wkcd->akd/dot_general | solution.py:41
  163.3 0.0 copy-done.1
  163.3 0.0 all-gather.11.cloned.1.call-update
  163.3 0.2 all-gather.13.cloned.1.call-start
  163.6 122.6 %all-gather.11.cloned.1.call-done = bf16[2048,8,256]{2,0,1:T(8,128)(2,1)} async-done(((bf16[256,8,256]{2,0,1:T(8,128)(2,1)}), bf16[2048,8,256]{2,0,1:T(8,128)(2,1)}) %all-gather.11.cloned.1.call-update) | async-done | bytes 8388624 | tf_op jit(solution)/shard_map/all_gather | solution.py:11
  286.1 4.9 reduce_sum.170
  291.1 2.4 fusion.64
  294.8 2.8 multiply_reduce_fusion.2
  298.2 2.9 divide_convert_fusion.2
  301.1 7.1 %fusion.120 = bf16[256,8,256]{2,0,1:T(8,128)(2,1)} fusion(bf16[256,8,256]{2,0,1:T(8,128)(2,1)} %divide_convert_fusion.2, bf16[1,4,8,256,256]{4,3,2,1,0:T(8,128)(2,1)} %param.6, bf16[1,4,8,256,256]{4,3,2,1,0:T(8,128)(2,1)} %param.5), kind=kOutput, calls=%fused_computation.121 | convolution fusion | flops 2150105088 | bytes 10485760 | tf_op jit(solution)/shard_map/wkac,wkcd->akd/dot_general | solution.py:41
  308.2 0.0 all-gather.13.cloned.1.call-update
  308.2 0.0 all-gather.15.cloned.1.call-start
  308.2 122.7 %all-gather.13.cloned.1.call-done = bf16[2048,8,256]{2,0,1:T(8,128)(2,1)} async-done(((bf16[256,8,256]{2,0,1:T(8,128)(2,1)}), bf16[2048,8,256]{2,0,1:T(8,128)(2,1)}) %all-gather.13.cloned.1.call-update) | async-done | bytes 8388624 | tf_op jit(solution)/shard_map/all_gather | solution.py:11
  431.0 6.1 reduce_sum.174
  437.1 2.8 fusion.67
  441.2 3.1 multiply_reduce_fusion.1
  445.0 3.2 divide_convert_fusion.1
  448.1 7.1 %fusion.127 = bf16[256,8,256]{2,0,1:T(8,128)(2,1)} fusion(bf16[256,8,256]{2,0,1:T(8,128)(2,1)} %divide_convert_fusion.1, bf16[1,4,8,256,256]{4,3,2,1,0:T(8,128)(2,1)} %param.6, bf16[1,4,8,256,256]{4,3,2,1,0:T(8,128)(2,1)} %param.5), kind=kOutput, calls=%fused_computation.122 | convolution fusion | flops 2150105088 | bytes 10485760 | tf_op jit(solution)/shard_map/wkac,wkcd->akd/dot_general | solution.py:41
  455.2 0.0 all-gather.15.cloned.1.call-update
  455.3 122.8 %all-gather.15.cloned.1.call-done = bf16[2048,8,256]{2,0,1:T(8,128)(2,1)} async-done(((bf16[256,8,256]{2,0,1:T(8,128)(2,1)}), bf16[2048,8,256]{2,0,1:T(8,128)(2,1)}) %all-gather.15.cloned.1.call-update) | async-done | bytes 8388624 | tf_op jit(solution)/shard_map/all_gather | solution.py:11
  578.1 6.2 reduce_sum.178
  584.2 2.8 fusion.70
  588.4 3.1 multiply_reduce_fusion
  592.1 9.0 %fusion = bf16[1,4,8,256,256]{3,4,1,2,0:T(8,128)(2,1)} fusion(bf16[256,8,256]{2,0,1:T(8,128)(2,1)} %reduce_sum.178, bf16[256,8,256]{2,0,1:T(8,128)(2,1)} %divide_convert_fusion.1, f32[]{:T(128)S(6)} %sqrt.19, f32[]{:T(128)S(6)} %div.139, f32[8,256]{1,0:T(8,128)S(1)} %fusion.147, f32[256,8]{0,1:T(8,128)S(1)} %fusion.148, bf16[1,4,8,256,256]{4,3,2,1,0:T(8,128)(2,1)} %param.5), kind=kOutput, calls=%fused_computation.12 | convolution fusion | flops 2164260864 | bytes 10502152 | tf_op jit(solution)/shard_map/gxah,hxe->gxae/dot_general | solution.py:56
  601.1 4.4 collective-permute-start
  605.5 8.1 %fusion.1 = bf16[1,4,8,256,256]{3,4,1,2,0:T(8,128)(2,1)} fusion(bf16[256,8,256]{2,0,1:T(8,128)(2,1)} %reduce_sum.178, bf16[256,8,256]{2,0,1:T(8,128)(2,1)} %divide_convert_fusion.1, f32[]{:T(128)S(6)} %sqrt.19, f32[]{:T(128)S(6)} %div.139, f32[8,256]{1,0:T(8,128)S(1)} %fusion.147, f32[256,8]{0,1:T(8,128)S(1)} %fusion.148, bf16[1,4,8,256,256]{4,3,2,1,0:T(8,128)(2,1)} %param.6), kind=kOutput, calls=%fused_computation.13 | convolution fusion | flops 2164260864 | bytes 10502152 | tf_op jit(solution)/shard_map/njpq,tjq->njpt/dot_general | solution.py:64
  613.6 2.1 collective-permute-start.1
  615.8 4.3 fusion.146
  620.1 31.2 %collective-permute-done = bf16[1,4,8,256,256]{3,4,1,2,0:T(8,128)(2,1)} collective-permute-done((bf16[1,4,8,256,256]{3,4,1,2,0:T(8,128)(2,1)}, bf16[1,4,8,256,256]{3,4,1,2,0:T(8,128)(2,1)}, u32[]{:S(2)}, u32[]{:S(2)}) %collective-permute-start) | collective-permute-done | bytes 4194336 | tf_op jit(solution)/shard_map/ppermute | solution.py:18
  651.3 6.2 copy.12
  657.4 6.3 collective-permute-done.1
  663.8 6.2 copy.13
Async XLA Ops:
  7.2 137.9 %all-gather.9.cloned.1.call-start = ((), (), s32[]{:S(2)}) async-start(), calls=%async_computation | async-start | bytes 9437184 | tf_op jit(solution)/shard_map/all_gather | solution.py:11
  19.1 267.1 %all-gather.11.cloned.1.call-start = ((), (), s32[]{:S(2)}) async-start(), calls=%async_computation.1 | async-start | bytes 9437184 | tf_op jit(solution)/shard_map/all_gather | solution.py:11
  145.0 5.0 copy-start
  156.2 7.2 %copy-start.1 = (bf16[256,8,256]{2,0,1:T(8,128)(2,1)}, bf16[256,8,256]{2,0,1:T(8,128)(2,1)S(1)}, u32[]{:S(2)}) copy-start(bf16[256,8,256]{2,0,1:T(8,128)(2,1)S(1)} %divide_convert_fusion.3) | copy-start | bytes 3145732
  163.3 267.6 %all-gather.13.cloned.1.call-start = ((), (), s32[]{:S(2)}) async-start(), calls=%async_computation.2 | async-start | bytes 9437184 | tf_op jit(solution)/shard_map/all_gather | solution.py:11
  308.2 269.9 %all-gather.15.cloned.1.call-start = ((), (), s32[]{:S(2)}) async-start(), calls=%async_computation.3 | async-start | bytes 9437184 | tf_op jit(solution)/shard_map/all_gather | solution.py:11
  601.1 50.1 %collective-permute-start = (bf16[1,4,8,256,256]{3,4,1,2,0:T(8,128)(2,1)}, bf16[1,4,8,256,256]{3,4,1,2,0:T(8,128)(2,1)}, u32[]{:S(2)}, u32[]{:S(2)}) collective-permute-start(bf16[1,4,8,256,256]{3,4,1,2,0:T(8,128)(2,1)} %fusion), channel_id=1, source_target_pairs={{0,8},{8,16},{16,24},{1,9},{9,17},{17,25},{2,10},{10,18},{18,26},{... | collective-permute-start | bytes 12582920 | tf_op jit(solution)/shard_map/ppermute | solution.py:18
  613.6 50.1 %collective-permute-start.1 = (bf16[1,4,8,256,256]{3,4,1,2,0:T(8,128)(2,1)}, bf16[1,4,8,256,256]{3,4,1,2,0:T(8,128)(2,1)}, u32[]{:S(2)}, u32[]{:S(2)}) collective-permute-start(bf16[1,4,8,256,256]{3,4,1,2,0:T(8,128)(2,1)} %fusion.1), channel_id=1, source_target_pairs={{8,0},{16,8},{24,16},{9,1},{17,9},{25,17},{10,2},{18,10},{26,18},{... | collective-permute-start | bytes 12582920 | tf_op jit(solution)/shard_map/ppermute | solution.py:18
Sparse Core Ops, SparseCore 0:
  19.2 125.7 all-gather.8
  163.5 122.6 all-gather.10
  308.3 122.6 all-gather.12
  455.4 122.6 all-gather.14
